TPU v7x, 512 devices: a whole 4x4x16 slice. The times are simulated.
512 devices in a mesh: dp: 16 (over y, z_hi, core), expert: 32 (over z_lo, x).
Axes of the slice: x: 4, y: 4, z: 16 (z_hi: 2, z_lo: 8; z = z_hi * 8 + z_lo), core: 2. Of those that a mesh axis runs over, the one named last changes fastest.
Arguments:
- tokens: bfloat16 [1536, 3584], P('dp', 'expert'), may hold values from -13 to 13
- routes: int32 [1536, 8], replicated, may hold values from 0 to 31, all different within a row; in each aligned block of 96 rows (0 to 95, 96 to 191, ...) at most 32 rows name the same one
- gate_weight: bfloat16 [32, 3584, 2048], P('expert', None, 'dp'), may hold values from -0.09375 to 0.09375
- up_weight: bfloat16 [32, 3584, 2048], P('expert', None, 'dp'), may hold values from -0.09375 to 0.09375
- hidden_grad: bfloat16 [32, 16, 32, 2048], P('expert', None, None, 'dp'), may hold values from -40 to 40
- clip_limit: float32 [32], P('expert'), may hold values from 1 to 40
Outputs:
- hidden: bfloat16 [32, 16, 32, 2048], P('expert', None, None, 'dp')
- grad_gate: bfloat16 [32, 3584, 2048], P('expert', None, 'dp')
- grad_up: bfloat16 [32, 3584, 2048], P('expert', None, 'dp')
- token_grad: bfloat16 [1536, 3584], P('dp', 'expert')
Inputs may be any that keep to these rules, and one draw needn't show every extreme that they name: `routes`: each row names 8 different experts. In each aligned block of 96 rows (the tokens of one index of dp) no expert is named by more than 32 rows, a bound that some block reaches.
All inputs are finite; a program needn't handle non-finite values.
Results may differ from a plain program's by a relative error of at most 0.014.
Values may be sent and summed in bfloat16 or wider, within the bound.
No kernel may reach another device: no remote copies, remote signals or barrier semaphores. Data moves between devices by JAX's collectives and lax.ppermute only.
A program may use at most 64 MiB of HBM per device.

v0:
```python
import jax
import jax.numpy as jnp
from jax import lax
from jax.sharding import PartitionSpec as P


def slot_tables(block_routes, experts, capacity, top_count):
    flat_routes = block_routes.reshape(-1)
    expert_ids = jnp.arange(experts, dtype=jnp.int32)
    onehot = (flat_routes[:, None] == expert_ids[None, :]).astype(jnp.int32)
    before = jnp.cumsum(onehot, axis=0) - onehot
    slot_ranks = jnp.sum(before * onehot, axis=1)
    owner_token = jnp.arange(flat_routes.shape[0], dtype=jnp.int32) // top_count
    token_of = (
        jnp.zeros((experts, capacity), jnp.int32).at[flat_routes, slot_ranks].set(owner_token)
    )
    occupied = jnp.zeros((experts, capacity), jnp.bool_).at[flat_routes, slot_ranks].set(True)
    return (slot_ranks.reshape(block_routes.shape), token_of, occupied)


def expert_math(row_block, grad_block, gate_w, up_w):
    gate_pre = jnp.dot(row_block, gate_w, preferred_element_type=jnp.float32)
    up_pre = jnp.dot(row_block, up_w, preferred_element_type=jnp.float32)
    sigma_gate = jax.nn.sigmoid(gate_pre)
    hidden_rows = (gate_pre * sigma_gate * up_pre).astype(jnp.bfloat16)
    grad_float = grad_block.astype(jnp.float32)
    up_act = (grad_float * gate_pre * sigma_gate).astype(jnp.bfloat16)
    gate_act = (grad_float * up_pre * sigma_gate * (1.0 + gate_pre * (1.0 - sigma_gate))).astype(
        jnp.bfloat16
    )
    over_rows = (((0,), (0,)), ((), ()))
    over_units = (((1,), (1,)), ((), ()))
    raw_gate = lax.dot_general(row_block, gate_act, over_rows, preferred_element_type=jnp.float32)
    raw_up = lax.dot_general(row_block, up_act, over_rows, preferred_element_type=jnp.float32)
    partial_value = lax.dot_general(
        gate_act, gate_w, over_units, preferred_element_type=jnp.float32
    )
    partial_value = partial_value + lax.dot_general(
        up_act, up_w, over_units, preferred_element_type=jnp.float32
    )
    return (hidden_rows, raw_gate, raw_up, partial_value)


def body(tokens, routes, gate_weight, up_weight, hidden_grad, clip_limit):
    dp_count = lax.axis_size("dp")
    expert_count = lax.axis_size("expert")
    local_experts = gate_weight.shape[0]
    experts = local_experts * expert_count
    capacity = hidden_grad.shape[2]
    hidden_units = gate_weight.shape[2]
    model_width = gate_weight.shape[1]
    top_count = routes.shape[1]
    tok_rows = tokens.shape[0]
    dp_index = lax.axis_index("dp")
    blocks = routes.reshape(dp_count, tok_rows, top_count)
    own_routes = lax.dynamic_index_in_dim(blocks, dp_index, 0, keepdims=False)
    slot_ranks, token_of, occupied = slot_tables(own_routes, experts, capacity, top_count)
    outgoing = jnp.where(occupied[:, :, None], tokens[token_of], jnp.zeros((), tokens.dtype))[
        :, None
    ]
    arrived = lax.all_to_all(outgoing, "expert", split_axis=0, concat_axis=3, tiled=True)
    gathered = lax.all_gather(arrived, "dp", axis=1, tiled=True)
    row_block = gathered[0].reshape(dp_count * capacity, model_width)
    grad_block = hidden_grad[0].reshape(dp_count * capacity, hidden_units)
    hidden_rows, raw_gate, raw_up, partial_value = expert_math(
        row_block, grad_block, gate_weight[0], up_weight[0]
    )
    hidden_list = [hidden_rows.reshape(dp_count, capacity, hidden_units)]
    gate_list = [raw_gate]
    up_list = [raw_up]
    partial_list = [partial_value.reshape(dp_count, capacity, model_width)]
    squares = [jnp.sum(raw_gate * raw_gate) + jnp.sum(raw_up * raw_up)]
    totals = lax.psum(jnp.stack(squares), "dp")
    root_mean = jnp.sqrt(totals / (2.0 * model_width * hidden_units * dp_count) + 1e-06)
    clip_scale = jnp.minimum(1.0, clip_limit / root_mean)
    grad_gate = (clip_scale[:, None, None] * jnp.stack(gate_list)).astype(jnp.bfloat16)
    grad_up = (clip_scale[:, None, None] * jnp.stack(up_list)).astype(jnp.bfloat16)
    hidden = jnp.stack(hidden_list)
    partials = jnp.stack(partial_list)
    own_sums = lax.psum_scatter(
        partials.astype(jnp.bfloat16), "dp", scatter_dimension=1, tiled=True
    ).astype(jnp.float32)
    returned = lax.all_to_all(
        own_sums.astype(jnp.bfloat16), "expert", split_axis=3, concat_axis=0, tiled=True
    ).astype(own_sums.dtype)
    flat_back = returned.reshape(experts * capacity, -1)
    picked = flat_back[own_routes * capacity + slot_ranks]
    token_grad = jnp.sum(picked, axis=1).astype(jnp.bfloat16)
    return (hidden, grad_gate, grad_up, token_grad)


def solution(mesh):
    placed = (
        P("dp", "expert"),
        P(),
        P("expert", None, "dp"),
        P("expert", None, "dp"),
        P("expert", None, None, "dp"),
        P("expert"),
    )
    return jax.shard_map(
        body,
        mesh=mesh,
        in_specs=placed,
        out_specs=(
            P("expert", None, None, "dp"),
            P("expert", None, "dp"),
            P("expert", None, "dp"),
            P("dp", "expert"),
        ),
        check_vma=False,
    )
```

profile of v0, /device:TPU:2, one launch (start us, length us, event | category | flops | bytes accessed | tf_op | source)
XLA Modules:
  0.0 447.1 jit_solution(14734203186781111919)
XLA Ops:
  7.2 1.1 copy.23
  8.7 1.7 reduce-window.6
  10.9 37.4 %scatter_fusion.1 = s32[32,32]{1,0:T(8,128)S(1)} fusion(s32[32,32]{1,0:T(8,128)S(1)} %broadcast.108, s32[768]{0:T(1024)S(1)} %fusion.22, s32[768]{0:T(1024)S(1)} %add_select_fusion), kind=kCustom, calls=%fused_computation.3 | custom fusion | bytes 15360 | tf_op jit(solution)/shard_map/scatter | solution.py:15
  48.5 38.1 %scatter_fusion = pred[32,32]{1,0:T(8,128)(4,1)S(1)} fusion(pred[32,32]{1,0:T(8,128)(4,1)S(1)} %broadcast_in_dim.18, s32[768]{0:T(1024)S(1)} %fusion.22, pred[768]{0:T(1024)(128)(4,1)S(1)} %broadcast.143), kind=kCustom, calls=%fused_computation.2 | custom fusion | bytes 8448 | tf_op jit(solution)/shard_map/scatter | solution.py:17
  86.5 3.2 gather_fusion
  90.0 33.5 %all_to_all.27 = bf16[32,1,32,112]{3,2,1,0:T(8,128)(2,1)S(1)} all-to-all(bf16[32,1,32,112]{3,2,1,0:T(8,128)(2,1)S(1)} %broadcast_select_fusion), channel_id=1, replica_groups=mesh['dp'=16,'expert'=32] {'expert'}, dimensions={0} | all-to-all | bytes 458752 | tf_op jit(solution)/shard_map/all_to_all | solution.py:61
  124.7 108.8 %all-gather.2.cloned.1.call-done = bf16[1,16,32,3584]{3,2,0,1:T(8,128)(2,1)} async-done(((bf16[1,1,32,3584]{3,2,0,1:T(8,128)(2,1)}), bf16[1,16,32,3584]{3,2,0,1:T(8,128)(2,1)}) %all-gather.2.cloned.1.call-update) | async-done | bytes 3670032 | tf_op jit(solution)/shard_map/all_gather | solution.py:62
  233.6 3.3 fusion.7
  236.9 1.8 fusion.11
  238.7 1.1 fusion.5
  239.8 2.9 add_convert_fusion
  243.6 4.0 multiply_reduce_fusion.1
  247.6 3.0 multiply_reduce_fusion
  251.9 68.3 %psum.7 = f32[1]{0:T(128)} all-reduce(f32[1]{0:T(128)} %bitcast.13), channel_id=1, replica_groups=mesh['dp'=16,'expert'=32] {'dp'}, use_global_device_ids=true, to_apply=%region_7.8 | all-reduce | flops 1 | bytes 8 | tf_op jit(solution)/shard_map/psum | solution.py:73
  320.9 60.3 %reduce-scatter.2.cloned.1.call-done = bf16[1,1,32,3584]{3,2,0,1:T(8,128)(2,1)} async-done(((bf16[1,16,32,3584]{3,2,0,1:T(8,128)(2,1)}), bf16[1,1,32,3584]{3,2,0,1:T(8,128)(2,1)}) %reduce-scatter.2.cloned.1.call-update) | async-done | bytes 229392 | tf_op jit(solution)/shard_map/reduce_scatter | solution.py:80
  381.2 4.4 copy.29
  386.1 21.6 %reduce.5 = bf16[3584,32]{1,0:T(8,128)(2,1)} reduce(bf16[3584,1,1,32]{3,2,1,0:T(2,128)(2,1)} %bitcast.89, bf16[]{:T(256)} %broadcast.167), dimensions={1,2}, to_apply=%bitcast.65.reduce_sub_computation | reduce | bytes 458754
  407.7 2.8 reshape.188
  410.5 5.1 %all-to-all-start.1 = ((bf16[32,2,1792]{2,1,0:T(2,128)(2,1)}), bf16[32,2,1792]{2,1,0:T(2,128)(2,1)S(1)}, u32[]{:S(2)}, u32[]{:S(2)}) async-start(bf16[32,2,1792]{2,1,0:T(2,128)(2,1)} %reshape.188), calls=%async_computation.2 | async-start | bytes 458752 | tf_op jit(solution)/shard_map/all_to_all | solution.py:83
  415.7 3.0 fusion
  418.7 12.9 %all-to-all-done.1 = bf16[32,2,1792]{2,1,0:T(2,128)(2,1)S(1)} async-done(((bf16[32,2,1792]{2,1,0:T(2,128)(2,1)}), bf16[32,2,1792]{2,1,0:T(2,128)(2,1)S(1)}, u32[]{:S(2)}, u32[]{:S(2)}) %all-to-all-start.1) | async-done | bytes 229408 | tf_op jit(solution)/shard_map/all_to_all | solution.py:83
  431.6 2.3 reshape.189
  433.9 3.5 bitcast_convert_fusion
  437.9 1.6 gather_fusion.1
  (42 shorter events, 4.3 us)
Async XLA Ops:
  7.2 229.7 %copy-start = (bf16[1,3584,128]{2,1,0:T(8,128)(2,1)S(1)}, bf16[1,3584,128]{2,1,0:T(8,128)(2,1)}, u32[]{:S(2)}) copy-start(bf16[1,3584,128]{2,1,0:T(8,128)(2,1)} %param.9) | copy-start | bytes 2752516
  7.2 226.4 %all-gather.2.cloned.1.call-start = ((), (), s32[]{:S(2)}) async-start(), calls=%async_computation.3 | async-start | bytes 3899392 | tf_op jit(solution)/shard_map/all_gather | solution.py:62
  10.9 75.6 %copy-start.1 = (bf16[96,112]{1,0:T(8,128)(2,1)S(1)}, bf16[96,112]{1,0:T(8,128)(2,1)}, u32[]{:S(2)}) copy-start(bf16[96,112]{1,0:T(8,128)(2,1)} %param.6) | copy-start | bytes 64516
  48.3 185.2 %copy-start.4 = (bf16[1,3584,128]{2,1,0:T(8,128)(2,1)S(1)}, bf16[1,3584,128]{2,1,0:T(8,128)(2,1)}, u32[]{:S(2)}) copy-start(bf16[1,3584,128]{2,1,0:T(8,128)(2,1)} %param.8) | copy-start | bytes 2752516
  89.8 147.1 %copy-start.5 = (bf16[1,16,32,128]{3,2,1,0:T(8,128)(2,1)S(1)}, bf16[1,16,32,128]{3,2,1,0:T(8,128)(2,1)}, u32[]{:S(2)}) copy-start(bf16[1,16,32,128]{3,2,1,0:T(8,128)(2,1)} %param.10) | copy-start | bytes 393220
  124.7 256.5 %reduce-scatter.2.cloned.1.call-start = ((), (), s32[]{:S(2)}) async-start(), calls=%async_computation.4 | async-start | bytes 3899392 | tf_op jit(solution)/shard_map/reduce_scatter | solution.py:80
  233.5 3.3 copy-start.2
  243.6 4.0 copy-start.3
  410.5 21.0 %all-to-all-start.1 = ((bf16[32,2,1792]{2,1,0:T(2,128)(2,1)}), bf16[32,2,1792]{2,1,0:T(2,128)(2,1)S(1)}, u32[]{:S(2)}, u32[]{:S(2)}) async-start(bf16[32,2,1792]{2,1,0:T(2,128)(2,1)} %reshape.188), calls=%async_computation.2 | async-start | bytes 458752 | tf_op jit(solution)/shard_map/all_to_all | solution.py:83
Sparse Core Ops, SparseCore 0:
  124.8 108.7 all-gather.1
  242.9 138.2 reduce-scatter.1
where the time goes:
time: 448 us; the launch traced here: 447 us
  waiting for transfers between devices  182 us (41%)
  blocking collectives  102 us (23%)
  local copies, waits for them, and re-layouts  93.9 us (21%)
  other arithmetic  31.1 us (7%)
  between operations  16.9 us (4%)
  matrix products  16.1 us (4%)
  starting transfers between devices  5.19 us (1%)
    all_gather x1, waiting for transfers between devices, body(): gathered = lax.all_gather(arrived, 'dp', axis=1, tiled=True)  109 us
    psum x1, blocking collectives, body(): totals = lax.psum(jnp.stack(squares), 'dp')  68.3 us
    reduce_scatter x1, waiting for transfers between devices, body(): lax.psum_scatter(partials.astype(jnp.bfloat16), 'dp', scatter_dimension=1...  60.3 us
    scatter x1, local copies, waits for them, and re-layouts, slot_tables(): jnp.zeros((experts, capacity), jnp.bool_).at[flat_routes, slot_ranks]  38.1 us
    scatter x1, local copies, waits for them, and re-layouts, slot_tables(): jnp.zeros((experts, capacity), jnp.int32).at[flat_routes, slot_ranks]  37.4 us
    all_to_all x1, blocking collectives, body(): lax.all_to_all(outgoing, 'expert', split_axis=0, concat_axis=3, tiled=True)  33.5 us
    unnamed x1, other arithmetic  21.6 us
    all_to_all x1, waiting for transfers between devices, body(): lax.all_to_all(own_sums.astype(jnp.bfloat16), 'expert', split_axis=3, con...  12.9 us
  transfers between devices with their start and end apart: 3, of which 3 were waited for; matrix products, arithmetic and copies ran while one was open for 2% of the time, Pallas kernels for 0%

commit v1 on v0

--- a/solution.py
+++ b/solution.py
@@ -59,7 +59,9 @@
         :, None
     ]
     arrived = lax.all_to_all(outgoing, "expert", split_axis=0, concat_axis=3, tiled=True)
-    gathered = lax.all_gather(arrived, "dp", axis=1, tiled=True)
+    gathered = jnp.concatenate(
+        lax.all_to_all(jnp.stack([arrived] * lax.axis_size("dp")), "dp", 0, 0), axis=1
+    )
     row_block = gathered[0].reshape(dp_count * capacity, model_width)
     grad_block = hidden_grad[0].reshape(dp_count * capacity, hidden_units)
     hidden_rows, raw_gate, raw_up, partial_value = expert_math(

time: 448 us -> 516 us (1.15)
  the two profiles are of different devices: /device:TPU:2 before, /device:TPU:8 now
where the time goes in v1:
time: 516 us; the launch traced here: 515 us
  blocking collectives  249 us (48%)
  waiting for transfers between devices  105 us (20%)
  local copies, waits for them, and re-layouts  93.6 us (18%)
  other arithmetic  31.1 us (6%)
  between operations  16.9 us (3%)
  matrix products  13.9 us (3%)
    all_to_all x1, blocking collectives, body(): lax.all_to_all(jnp.stack([arrived] * lax.axis_size('dp')), 'dp', 0, 0)  153 us
    reduce_scatter x1, waiting for transfers between devices, body(): lax.psum_scatter(partials.astype(jnp.bfloat16), 'dp', scatter_dimension=1...  91.2 us
    psum x1, blocking collectives, body(): totals = lax.psum(jnp.stack(squares), 'dp')  61.6 us
    scatter x1, local copies, waits for them, and re-layouts, slot_tables(): jnp.zeros((experts, capacity), jnp.bool_).at[flat_routes, slot_ranks]  38.1 us
    scatter x1, local copies, waits for them, and re-layouts, slot_tables(): jnp.zeros((experts, capacity), jnp.int32).at[flat_routes, slot_ranks]  37.4 us
    all_to_all x1, blocking collectives, body(): lax.all_to_all(outgoing, 'expert', split_axis=0, concat_axis=3, tiled=True)  34.4 us
    unnamed x1, other arithmetic  21.6 us
    all_to_all x1, waiting for transfers between devices, body(): lax.all_to_all(own_sums.astype(jnp.bfloat16), 'expert', split_axis=3, con...  13.8 us
  transfers between devices with their start and end apart: 2, of which 2 were waited for; matrix products, arithmetic and copies ran while one was open for 2% of the time, Pallas kernels for 0%

profile of v1, /device:TPU:8, one launch (start us, length us, event | category | flops | bytes accessed | tf_op | source)
XLA Modules:
  0.0 514.8 jit_solution(12661837331516988620)
XLA Ops:
  7.2 1.1 copy.22
  8.7 1.7 reduce-window.6
  10.9 37.4 %scatter_fusion.1 = s32[32,32]{1,0:T(8,128)S(1)} fusion(s32[32,32]{1,0:T(8,128)S(1)} %broadcast.110, s32[768]{0:T(1024)S(1)} %fusion.22, s32[768]{0:T(1024)S(1)} %add_select_fusion), kind=kCustom, calls=%fused_computation.3 | custom fusion | bytes 15360 | tf_op jit(solution)/shard_map/scatter | solution.py:15
  48.5 38.1 %scatter_fusion = pred[32,32]{1,0:T(8,128)(4,1)S(1)} fusion(pred[32,32]{1,0:T(8,128)(4,1)S(1)} %broadcast_in_dim.18, s32[768]{0:T(1024)S(1)} %fusion.22, pred[768]{0:T(1024)(128)(4,1)S(1)} %broadcast.145), kind=kCustom, calls=%fused_computation.2 | custom fusion | bytes 8448 | tf_op jit(solution)/shard_map/scatter | solution.py:17
  86.5 3.2 gather_fusion
  90.0 34.4 %all_to_all.29 = bf16[32,1,32,112]{3,2,1,0:T(8,128)(2,1)S(1)} all-to-all(bf16[32,1,32,112]{3,2,1,0:T(8,128)(2,1)S(1)} %broadcast_select_fusion), channel_id=1, replica_groups=mesh['dp'=16,'expert'=32] {'expert'}, dimensions={0} | all-to-all | bytes 458752 | tf_op jit(solution)/shard_map/all_to_all | solution.py:61
  125.2 153.4 %all_to_all.30 = bf16[16,1,1,32,3584]{4,3,2,1,0:T(8,128)(2,1)S(1)} all-to-all(bf16[16,1,1,32,3584]{4,3,2,1,0:T(8,128)(2,1)S(1)} %stack.7), channel_id=1, replica_groups=mesh['dp'=16,'expert'=32] {'dp'}, dimensions={0} | all-to-all | bytes 7340032 | tf_op jit(solution)/shard_map/all_to_all | solution.py:63
  278.6 1.1 fusion.7
  279.7 1.8 fusion.11
  281.5 1.1 fusion.5
  282.7 2.9 add_convert_fusion
  286.5 3.9 multiply_reduce_fusion.1
  290.5 3.0 multiply_reduce_fusion
  294.8 61.6 %psum.7 = f32[1]{0:T(128)} all-reduce(f32[1]{0:T(128)} %bitcast.12), channel_id=1, replica_groups=mesh['dp'=16,'expert'=32] {'dp'}, use_global_device_ids=true, to_apply=%region_7.8 | all-reduce | flops 1 | bytes 8 | tf_op jit(solution)/shard_map/psum | solution.py:75
  357.1 91.2 %reduce-scatter.2.cloned.1.call-done = bf16[1,1,32,3584]{3,2,0,1:T(8,128)(2,1)} async-done(((bf16[1,16,32,3584]{3,2,0,1:T(8,128)(2,1)}), bf16[1,1,32,3584]{3,2,0,1:T(8,128)(2,1)}) %reduce-scatter.2.cloned.1.call-update) | async-done | bytes 229392 | tf_op jit(solution)/shard_map/reduce_scatter | solution.py:82
  448.3 4.4 copy.27
  453.2 21.6 %reduce.5 = bf16[3584,32]{1,0:T(8,128)(2,1)} reduce(bf16[3584,1,1,32]{3,2,1,0:T(2,128)(2,1)} %bitcast.88, bf16[]{:T(256)} %broadcast.169), dimensions={1,2}, to_apply=%bitcast.64.reduce_sub_computation | reduce | bytes 458754
  474.9 2.8 reshape.193
  477.7 4.8 all-to-all-start.2
  482.5 3.0 fusion
  485.5 13.8 %all-to-all-done.2 = bf16[32,2,1792]{2,1,0:T(2,128)(2,1)S(1)} async-done(((bf16[32,2,1792]{2,1,0:T(2,128)(2,1)}), bf16[32,2,1792]{2,1,0:T(2,128)(2,1)S(1)}, u32[]{:S(2)}, u32[]{:S(2)}) %all-to-all-start.2) | async-done | bytes 229408 | tf_op jit(solution)/shard_map/all_to_all | solution.py:85
  499.3 2.3 reshape.194
  501.6 3.5 bitcast_convert_fusion
  505.7 1.6 gather_fusion.1
  (41 shorter events, 3.8 us)
Async XLA Ops:
  7.2 272.6 %copy-start = (bf16[1,3584,128]{2,1,0:T(8,128)(2,1)S(1)}, bf16[1,3584,128]{2,1,0:T(8,128)(2,1)}, u32[]{:S(2)}) copy-start(bf16[1,3584,128]{2,1,0:T(8,128)(2,1)} %param.9) | copy-start | bytes 2752516
  7.2 441.1 %reduce-scatter.2.cloned.1.call-start = ((), (), s32[]{:S(2)}) async-start(), calls=%async_computation.4 | async-start | bytes 3899392 | tf_op jit(solution)/shard_map/reduce_scatter | solution.py:82
  10.9 75.6 %copy-start.1 = (bf16[96,112]{1,0:T(8,128)(2,1)S(1)}, bf16[96,112]{1,0:T(8,128)(2,1)}, u32[]{:S(2)}) copy-start(bf16[96,112]{1,0:T(8,128)(2,1)} %param.6) | copy-start | bytes 64516
  125.2 153.4 %copy-start.4 = (bf16[1,3584,128]{2,1,0:T(8,128)(2,1)S(1)}, bf16[1,3584,128]{2,1,0:T(8,128)(2,1)}, u32[]{:S(2)}) copy-start(bf16[1,3584,128]{2,1,0:T(8,128)(2,1)} %param.8) | copy-start | bytes 2752516
  278.6 2.9 copy-start.2
  278.6 1.1 copy-start.5
  286.5 4.0 copy-start.3
  477.7 21.6 %all-to-all-start.2 = ((bf16[32,2,1792]{2,1,0:T(2,128)(2,1)}), bf16[32,2,1792]{2,1,0:T(2,128)(2,1)S(1)}, u32[]{:S(2)}, u32[]{:S(2)}) async-start(bf16[32,2,1792]{2,1,0:T(2,128)(2,1)} %reshape.193), calls=%async_computation.3 | async-start | bytes 458752 | tf_op jit(solution)/shard_map/all_to_all | solution.py:85
Sparse Core Ops, SparseCore 0:
  285.8 162.5 reduce-scatter.1
